TPU v7x, 32 devices: a whole 2x2x4 slice. The times are simulated.
32 devices in a mesh: dp: 4 (over y, x), expert: 8 (over z, core).
Axes of the slice: x: 2, y: 2, z: 4, core: 2. Of those that a mesh axis runs over, the one named last changes fastest.
Arguments:
- saved_input: bfloat16 [1024, 2048], P(('dp', 'expert')), may hold values from -6 to 6
- output_grad: bfloat16 [1024, 2048], P(('dp', 'expert')), may hold values from -6 to 6
- route_probs: float32 [1024, 8], P(('dp', 'expert')), may hold values from 0.02 to 0.4
- expert_choice: int32 [1024, 8], P(('dp', 'expert')), may hold values from 0 to 15, all different within a row; in each aligned block of 32 rows (0 to 31, 32 to 63, ...) at most 24 rows name the same one
- slot_expert: int32 [4, 8], replicated, may hold values from 0 to 15, as said below
- frozen_gate: bfloat16 [32, 2048, 768], P(('dp', 'expert')), as said below
- frozen_up: bfloat16 [32, 2048, 768], P(('dp', 'expert')), as said below
- frozen_down: bfloat16 [32, 768, 2048], P(('dp', 'expert')), as said below
- adapter_in: float32 [16, 64, 768], P('expert', 'dp'), may hold values from -0.21875 to 0.21875
- adapter_out: float32 [16, 64, 2048], P('expert', 'dp'), may hold values from -0.125 to 0.125
- moment_in: float32 [16, 64, 768], P('expert', 'dp'), may hold values from -3 to 3
- moment_out: float32 [16, 64, 2048], P('expert', 'dp'), may hold values from -3 to 3
- second_in: float32 [16, 64, 768], P('expert', 'dp'), may hold values from 0.01 to 1
- second_out: float32 [16, 64, 2048], P('expert', 'dp'), may hold values from 0.01 to 1
Outputs:
- input_grad: bfloat16 [1024, 2048], P(('dp', 'expert'))
- step_in: float32 [16, 64, 768], P('expert', 'dp')
- step_out: float32 [16, 64, 2048], P('expert', 'dp')
- momentum_in: float32 [16, 64, 768], P('expert', 'dp')
- momentum_out: float32 [16, 64, 2048], P('expert', 'dp')
- variance_in: float32 [16, 64, 768], P('expert', 'dp')
- variance_out: float32 [16, 64, 2048], P('expert', 'dp')
- replica_in: bfloat16 [32, 64, 768], P(('dp', 'expert'))
- replica_out: bfloat16 [32, 64, 2048], P(('dp', 'expert'))
Inputs may be any that keep to these rules, and one draw needn't show every extreme that they name: `expert_choice`: among the rows of one device no expert is named more than 24 times. `slot_expert`: the slots of index j of the expert axis host only experts 2 * j to 2 * j + 1, and each of these at least once. `frozen_gate`: slots that host the same expert hold the same frozen weights. `frozen_up`: slots that host the same expert hold the same frozen weights. `frozen_down`: slots that host the same expert hold the same frozen weights.
All inputs are finite; a program needn't handle non-finite values.
Results may differ from a plain program's by a relative error of at most 0.012.
Values may be sent and summed in bfloat16 or wider, within the bound.
No kernel may reach another device: no remote copies, remote signals or barrier semaphores. Data moves between devices by JAX's collectives and lax.ppermute only.
A program may use at most 128 MiB of HBM per device.

v0:
```python
import jax
import jax.numpy as jnp
from jax import lax
from jax.sharding import PartitionSpec as P

STEP = 100
adapter_scale_factor = 2.0
beta_one = 0.9
beta_two = 0.999
decay_rate = 0.01
adam_eps = 1e-08


def contract_product(left, right, left_dim, right_dim):
    return lax.dot_general(
        left, right, (((left_dim,), (right_dim,)), ((), ())), preferred_element_type=jnp.float32
    )


def route_rows(choice_flat, slot_expert, source, local_experts):
    column = choice_flat // local_experts
    hosted = (jnp.take(slot_expert, column, axis=1) == choice_flat[None, :]).astype(jnp.int32)
    counts = jnp.sum(hosted, axis=0)
    picked = source % counts
    running = jnp.cumsum(hosted, axis=0) - 1
    chosen = hosted * (running == picked[None, :]).astype(jnp.int32)
    dp_ids = jnp.arange(hosted.shape[0], dtype=jnp.int32)
    dest_row = jnp.sum(chosen * dp_ids[:, None], axis=0)
    row_ids = jnp.arange(choice_flat.shape[0], dtype=jnp.int32)
    earlier = (choice_flat[None, :] == choice_flat[:, None]) & (row_ids[None, :] < row_ids[:, None])
    rank = jnp.sum(earlier.astype(jnp.int32), axis=1)
    return (dest_row, column, rank)


def pack_rows(saved_input, scaled, position, buffer_size, top_count, shape_out):
    row_count = scaled.shape[0]
    row_ids = jnp.arange(row_count, dtype=jnp.int32)
    filler = jnp.full((buffer_size,), row_count, jnp.int32).at[position].set(row_ids)
    send_input = jnp.take(saved_input, filler // top_count, axis=0, mode="fill", fill_value=0)
    send_grad = jnp.take(scaled, filler, axis=0, mode="fill", fill_value=0)
    return (send_input.reshape(shape_out), send_grad.reshape(shape_out))


def adamw(param, grad, first, second):
    first_new = beta_one * first + (1.0 - beta_one) * grad
    second_new = beta_two * second + (1.0 - beta_two) * grad * grad
    corr_one = 1.0 - beta_one**STEP
    corr_two = 1.0 - beta_two**STEP
    step_dir = (
        first_new / corr_one / (jnp.sqrt(second_new / corr_two) + adam_eps) + decay_rate * param
    )
    return (step_dir, first_new, second_new)


def per_device(
    saved_input,
    output_grad,
    route_probs,
    expert_choice,
    slot_expert,
    frozen_gate,
    frozen_up,
    frozen_down,
    adapter_in,
    adapter_out,
    moment_in,
    moment_out,
    second_in,
    second_out,
):
    dp_count = lax.axis_size("dp")
    expert_count = lax.axis_size("expert")
    dp_index = lax.axis_index("dp")
    column_index = lax.axis_index("expert")
    local_experts = adapter_in.shape[0]
    token_count, top_count = expert_choice.shape
    width = saved_input.shape[1]
    row_count = token_count * top_count
    capacity = max(2, -(-3 * row_count // (2 * local_experts * expert_count)))
    buffer_size = dp_count * expert_count * capacity
    source = dp_index * expert_count + column_index
    choice_flat = expert_choice.reshape(row_count)
    dest_row, column, rank = route_rows(choice_flat, slot_expert, source, local_experts)
    scaled = (
        (route_probs[:, :, None] * output_grad[:, None, :].astype(jnp.float32))
        .astype(jnp.bfloat16)
        .reshape(row_count, width)
    )
    col_size = local_experts * expert_count * capacity
    col_position = (choice_flat % local_experts * expert_count + column) * capacity + rank
    col_shape = (local_experts, expert_count, capacity, width)
    col_input, col_grad = pack_rows(
        saved_input, scaled, col_position, col_size, top_count, col_shape
    )
    got_input, got_grad = (
        lax.all_to_all(col_input, "expert", split_axis=1, concat_axis=1, tiled=True),
        lax.all_to_all(col_grad, "expert", split_axis=1, concat_axis=1, tiled=True),
    )
    column_hosts = lax.dynamic_index_in_dim(slot_expert, column_index, 1, keepdims=False)
    dp_ids = jnp.arange(dp_count, dtype=jnp.int32)
    same_host = (column_hosts[:, None] == column_hosts[None, :]).astype(jnp.int32)
    host_count = jnp.sum(same_host, axis=1)
    host_place = jnp.sum(same_host * (dp_ids[None, :] < dp_ids[:, None]).astype(jnp.int32), axis=1)
    sources = dp_index * expert_count + jnp.arange(expert_count, dtype=jnp.int32)
    serves = sources[None, :] % host_count[:, None] == host_place[:, None]
    local_of = column_hosts - local_experts * column_index
    kept_mask = serves[:, :, None, None]
    zero_value = jnp.zeros((), jnp.bfloat16)
    picked_input = jnp.where(kept_mask, jnp.take(got_input, local_of, axis=0), zero_value)
    picked_grad = jnp.where(kept_mask, jnp.take(got_grad, local_of, axis=0), zero_value)
    arrived_input, arrived_grad = (
        lax.all_to_all(picked_input, "dp", split_axis=0, concat_axis=0, tiled=True),
        lax.all_to_all(picked_grad, "dp", split_axis=0, concat_axis=0, tiled=True),
    )
    fetched_in, fetched_out = (
        lax.all_gather(adapter_in.astype(jnp.bfloat16), "dp", axis=1, tiled=True),
        lax.all_gather(adapter_out.astype(jnp.bfloat16), "dp", axis=1, tiled=True),
    )
    hosted_local = slot_expert[dp_index, column_index] - local_experts * column_index
    owned_input = lax.dynamic_index_in_dim(fetched_in, hosted_local, 0, keepdims=False)
    own_out = lax.dynamic_index_in_dim(fetched_out, hosted_local, 0, keepdims=False)
    buffer_rows = arrived_input.reshape(buffer_size, width)
    gradient_row_block = arrived_grad.reshape(buffer_size, width)
    gate_weight = frozen_gate[0]
    up_weight = frozen_up[0]
    down_weight = frozen_down[0]
    gate_pre = jnp.dot(buffer_rows, gate_weight, preferred_element_type=jnp.float32)
    up_pre = jnp.dot(buffer_rows, up_weight, preferred_element_type=jnp.float32)
    sigmoid_gate = jax.nn.sigmoid(gate_pre)
    hidden_state = (gate_pre * sigmoid_gate * up_pre).astype(jnp.bfloat16)
    low_rank_input = contract_product(hidden_state, owned_input, 1, 1).astype(jnp.bfloat16)
    low_rank_gradient = contract_product(gradient_row_block, own_out, 1, 1).astype(jnp.bfloat16)
    hidden_gradient = contract_product(gradient_row_block, down_weight, 1, 1)
    hidden_gradient = hidden_gradient + adapter_scale_factor * jnp.dot(
        low_rank_gradient, owned_input, preferred_element_type=jnp.float32
    )
    up_grad = (hidden_gradient * gate_pre * sigmoid_gate).astype(jnp.bfloat16)
    gate_grad = (
        hidden_gradient * up_pre * sigmoid_gate * (1.0 + gate_pre * (1.0 - sigmoid_gate))
    ).astype(jnp.bfloat16)
    back_rows = (
        contract_product(gate_grad, gate_weight, 1, 1) + contract_product(up_grad, up_weight, 1, 1)
    ).astype(jnp.bfloat16)
    incoming_gradient = adapter_scale_factor * contract_product(
        low_rank_gradient, hidden_state, 0, 0
    )
    outgoing_gradient = adapter_scale_factor * contract_product(
        low_rank_input, gradient_row_block, 0, 0
    )
    back_block = back_rows.reshape(dp_count, expert_count, capacity, width)
    came_back = lax.all_to_all(back_block, "dp", split_axis=0, concat_axis=0, tiled=True)
    pieces_back = []
    for which_local in range(local_experts):
        chosen_mask = (serves & (local_of == which_local)[:, None])[:, :, None, None]
        pieces_back.append(jnp.sum(jnp.where(chosen_mask, came_back, zero_value), axis=0))
    gone_back = lax.all_to_all(
        jnp.stack(pieces_back), "expert", split_axis=1, concat_axis=1, tiled=True
    )
    per_row = jnp.take(gone_back.reshape(col_size, width), col_position, axis=0)
    input_grad = jnp.sum(
        per_row.reshape(token_count, top_count, width).astype(jnp.float32), axis=1
    ).astype(jnp.bfloat16)
    selector = (jnp.arange(local_experts, dtype=jnp.int32) == hosted_local).astype(jnp.float32)
    placed_in = selector[:, None, None] * incoming_gradient[None, :, :]
    placed_out = selector[:, None, None] * outgoing_gradient[None, :, :]
    summed_in, summed_out = (
        lax.psum_scatter(placed_in, "dp", scatter_dimension=1, tiled=True),
        lax.psum_scatter(placed_out, "dp", scatter_dimension=1, tiled=True),
    )
    step_in, momentum_in, variance_in = adamw(adapter_in, summed_in, moment_in, second_in)
    step_out, momentum_out, variance_out = adamw(adapter_out, summed_out, moment_out, second_out)
    copied_in, copied_out = (
        lax.all_gather(step_in.astype(jnp.bfloat16), "dp", axis=1, tiled=True),
        lax.all_gather(step_out.astype(jnp.bfloat16), "dp", axis=1, tiled=True),
    )
    replica_in = lax.dynamic_index_in_dim(copied_in, hosted_local, 0, keepdims=True)
    replica_out = lax.dynamic_index_in_dim(copied_out, hosted_local, 0, keepdims=True)
    return (
        input_grad,
        step_in,
        step_out,
        momentum_in,
        momentum_out,
        variance_in,
        variance_out,
        replica_in,
        replica_out,
    )


def solution(mesh):
    return jax.shard_map(
        per_device,
        mesh=mesh,
        in_specs=(
            P(("dp", "expert"), None),
            P(("dp", "expert"), None),
            P(("dp", "expert"), None),
            P(("dp", "expert"), None),
            P(),
            P(("dp", "expert"), None, None),
            P(("dp", "expert"), None, None),
            P(("dp", "expert"), None, None),
            P("expert", "dp", None),
            P("expert", "dp", None),
            P("expert", "dp", None),
            P("expert", "dp", None),
            P("expert", "dp", None),
            P("expert", "dp", None),
        ),
        out_specs=(
            P(("dp", "expert"), None),
            P("expert", "dp", None),
            P("expert", "dp", None),
            P("expert", "dp", None),
            P("expert", "dp", None),
            P("expert", "dp", None),
            P("expert", "dp", None),
            P(("dp", "expert"), None, None),
            P(("dp", "expert"), None, None),
        ),
        check_vma=False,
    )
```

profile of v0, /device:TPU:0, one launch (start us, length us, event | category | flops | bytes accessed | tf_op | source)
XLA Modules:
  0.0 375.1 jit_solution(5800526938693478548)
XLA Ops:
  7.2 0.9 copy.53
  8.1 0.1 reshape.475
  8.2 0.1 reshape.476
  8.3 0.2 convert_reduce_fusion
  8.5 0.5 copy-done.9
  9.1 1.4 scatter_custom_fusion
  10.5 0.1 broadcast_in_dim.106
  10.6 6.0 %gather_fusion.1 = bf16[384,2048]{1,0:T(8,128)(2,1)} fusion(bf16[32,2048]{1,0:T(8,128)(2,1)} %param.16, s32[1024]{0:T(1024)S(1)} %pad_clamp_fusion.1), kind=kCustom, calls=%fused_computation.3 | custom fusion | bytes 3147264 | tf_op jit(solution)/shard_map/jit(_take)/gather | solution.py:39
  16.6 2.8 copy_select_fusion
  19.4 6.5 %all-to-all-start.2 = ((bf16[2,8,24,2048]{3,2,0,1:T(8,128)(2,1)}), bf16[2,8,24,2048]{3,2,0,1:T(8,128)(2,1)}, u32[]{:S(2)}, u32[]{:S(2)}) async-start(bf16[2,8,24,2048]{3,2,0,1:T(8,128)(2,1)} %copy_select_fusion), calls=%async_computation.2 | async-start | bytes 3145728 | tf_op jit(solution)/shard_map/all_to_all | solution.py:96
  25.8 0.1 broadcast_in_dim.101
  25.9 0.6 copy.59
  26.6 0.8 copy.60
  27.3 0.1 mul.213
  27.4 0.7 add_select_fusion.3
  28.1 1.2 fusion.9
  29.3 6.4 %gather_fusion = bf16[384,2048]{1,0:T(8,128)(2,1)} fusion(bf16[256,2048]{1,0:T(8,128)(2,1)} %fusion.9, s32[1024]{0:T(1024)S(1)} %pad_clamp_fusion.3), kind=kCustom, calls=%fused_computation.2 | custom fusion | bytes 3147264 | tf_op jit(solution)/shard_map/jit(_take)/gather | solution.py:40
  35.8 2.8 copy_select_fusion.1
  38.5 25.2 %all-to-all-done.2 = bf16[2,8,24,2048]{3,2,0,1:T(8,128)(2,1)} async-done(((bf16[2,8,24,2048]{3,2,0,1:T(8,128)(2,1)}), bf16[2,8,24,2048]{3,2,0,1:T(8,128)(2,1)}, u32[]{:S(2)}, u32[]{:S(2)}) %all-to-all-start.2) | async-done | bytes 1572896 | tf_op jit(solution)/shard_map/all_to_all | solution.py:96
  63.8 4.3 %all-to-all-start = ((bf16[2,8,24,2048]{3,2,0,1:T(8,128)(2,1)}), bf16[2,8,24,2048]{3,2,0,1:T(8,128)(2,1)}, u32[]{:S(2)}, u32[]{:S(2)}) async-start(bf16[2,8,24,2048]{3,2,0,1:T(8,128)(2,1)} %copy_select_fusion.1), calls=%async_computation | async-start | bytes 3145728 | tf_op jit(solution)/shard_map/all_to_all | solution.py:97
  68.1 0.2 fusion.42
  68.3 0.7 compare_reduce_fusion.1
  69.0 0.2 convert_reduce_fusion.1
  69.2 0.7 broadcast_and_fusion
  69.9 3.8 %gather_fusion.4 = bf16[4,8,24,2048]{3,2,1,0:T(8,128)(2,1)} fusion(bf16[2,8,24,2048]{3,2,0,1:T(8,128)(2,1)} %all-to-all-done.2, s32[1024]{0:T(1024)S(1)} %pad_clamp_fusion.2), kind=kCustom, calls=%fused_computation.1.clone | custom fusion | bytes 6291472 | tf_op jit(solution)/shard_map/jit(_take)/gather | solution.py:109
  73.7 32.2 %all-to-all-done = bf16[2,8,24,2048]{3,2,0,1:T(8,128)(2,1)} async-done(((bf16[2,8,24,2048]{3,2,0,1:T(8,128)(2,1)}), bf16[2,8,24,2048]{3,2,0,1:T(8,128)(2,1)}, u32[]{:S(2)}, u32[]{:S(2)}) %all-to-all-start) | async-done | bytes 1572896 | tf_op jit(solution)/shard_map/all_to_all | solution.py:97
  105.9 3.9 %gather_fusion.3 = bf16[4,8,24,2048]{3,2,1,0:T(8,128)(2,1)} fusion(bf16[2,8,24,2048]{3,2,0,1:T(8,128)(2,1)} %all-to-all-done, s32[1024]{0:T(1024)S(1)} %pad_clamp_fusion.2), kind=kCustom, calls=%fused_computation.clone | custom fusion | bytes 6291472 | tf_op jit(solution)/shard_map/jit(_take)/gather | solution.py:110
  109.7 5.3 %select_select_fusion.1 = (bf16[4,8,24,2048]{3,2,1,0:T(8,128)(2,1)}, bf16[4,8,24,2048]{3,2,1,0:T(8,128)(2,1)S(1)}) fusion(bf16[4,8,24,2048]{3,2,1,0:T(8,128)(2,1)} %gather_fusion.3, pred[4]{0:T(512)(128)(4,1)S(1)} %get-tuple-element.26, pred[4,8]{1,0:T(4,128)(4,1)S(1)} %get-tuple-element.25, bf16[4,8,24,2048]{3,2,1,0:T(8,128)(2,1)} %gather_fusion.4), kind=kLoop, calls=%fused_computation.17 | loop fusion | flops 6291456 | bytes 12582948 | tf_op jit(solution)/shard_map/jit(_where)/select_n | solution.py:110
  115.0 39.9 %all_to_all.30 = bf16[4,8,24,2048]{3,2,1,0:T(8,128)(2,1)} all-to-all(bf16[4,8,24,2048]{3,2,1,0:T(8,128)(2,1)S(1)} %get-tuple-element.33), channel_id=1, replica_groups=mesh['dp'=4,'expert'=8] {'dp'}, dimensions={0} | all-to-all | bytes 6291456 | tf_op jit(solution)/shard_map/all_to_all | solution.py:112
  155.0 4.8 %all-to-all-start.1 = ((bf16[4,8,24,2048]{3,2,1,0:T(8,128)(2,1)}), bf16[4,8,24,2048]{3,2,1,0:T(8,128)(2,1)}, u32[]{:S(2)}, u32[]{:S(2)}) async-start(bf16[4,8,24,2048]{3,2,1,0:T(8,128)(2,1)} %get-tuple-element.32), calls=%async_computation.1 | async-start | bytes 6291456 | tf_op jit(solution)/shard_map/all_to_all | solution.py:113
  159.8 0.6 dynamic_slice.24
  161.1 37.8 %all_gather.13 = bf16[2,64,768]{2,1,0:T(8,128)(2,1)S(1)} all-gather(bf16[2,16,768]{2,1,0:T(8,128)(2,1)S(1)} %convert_element_type.64), channel_id=1, replica_groups=mesh['dp'=4,'expert'=8] {'dp'}, dimensions={1}, use_global_device_ids=true | all-gather | bytes 245760 | tf_op jit(solution)/shard_map/all_gather | solution.py:116
  199.0 5.6 %fusion.2 = f32[768,768]{1,0:T(8,128)S(1)} fusion(bf16[768,2048]{1,0:T(8,128)(2,1)} %bitcast.55, bf16[1,2048,768]{2,1,0:T(8,128)(2,1)} %param.21), kind=kOutput, calls=%fused_computation.9 | convolution fusion | flops 2415919104 | bytes 8650752 | tf_op jit(solution)/shard_map/dot_general | solution.py:127
  204.6 1.4 copy-done.20
  206.0 4.5 %multiply_convert_fusion = (bf16[768,768]{1,0:T(8,128)(2,1)}, f32[768,768]{1,0:T(8,128)}) fusion(f32[768,768]{1,0:T(8,128)S(1)} %fusion.2, bf16[768,2048]{1,0:T(8,128)(2,1)S(1)} %bitcast.56, bf16[1,2048,768]{2,1,0:T(8,128)(2,1)S(1)} %copy-done), kind=kOutput, calls=%fused_computation.20 | convolution fusion | flops 2419458048 | bytes 12189696 | tf_op jit(solution)/shard_map/dot_general | solution.py:128
  210.5 4.3 %convolution_multiply_fusion = f32[64,2048]{1,0:T(8,128)} fusion(bf16[768,2048]{1,0:T(8,128)(2,1)} %bitcast.4, bf16[768,768]{1,0:T(8,128)(2,1)} %get-tuple-element.34, bf16[2,64,768]{2,1,0:T(8,128)(2,1)S(1)} %all_gather.13, s32[]{:T(128)S(6)} %select_n.159), kind=kOutput, calls=%fused_computation.25 | convolution fusion | flops 277004288 | bytes 4947972 | tf_op jit(solution)/shard_map/dot_general | solution.py:15
  214.8 2.2 broadcast_multiply_fusion
  217.0 6.9 %fusion.7 = f32[768,768]{1,0:T(8,128)} fusion(bf16[768,2048]{1,0:T(8,128)(2,1)} %bitcast.4, bf16[1,768,2048]{2,1,0:T(8,128)(2,1)} %param.23), kind=kOutput, calls=%fused_computation.14 | convolution fusion | flops 2415919104 | bytes 8650752 | tf_op jit(solution)/shard_map/dot_general | solution.py:15
  223.9 20.0 %reduce-scatter.5.cloned.1.call-done = f32[2,16,2048]{2,1,0:T(8,128)} async-done(((f32[2,64,2048]{2,1,0:T(8,128)}), f32[2,16,2048]{2,1,0:T(8,128)}) %reduce-scatter.5.cloned.1.call-update) | async-done | bytes 262160 | tf_op jit(solution)/shard_map/reduce_scatter | solution.py:168
  243.9 2.3 fusion.49
  246.2 10.3 %all_gather.12 = bf16[2,64,2048]{2,1,0:T(8,128)(2,1)S(1)} all-gather(bf16[2,16,2048]{2,1,0:T(8,128)(2,1)S(1)} %get-tuple-element.30), channel_id=1, replica_groups=mesh['dp'=4,'expert'=8] {'dp'}, dimensions={1}, use_global_device_ids=true | all-gather | bytes 655360 | tf_op jit(solution)/shard_map/all_gather | solution.py:117
  256.5 3.1 convolution_convert_fusion.1
  259.6 0.5 multiply_add_fusion
  260.1 0.4 copy-done.22
  260.5 1.2 copy-done.19
  261.7 3.3 fusion
  265.0 4.2 %add_convert_fusion = bf16[768,2048]{1,0:T(8,128)(2,1)} fusion(f32[768,2048]{1,0:T(8,128)S(1)} %fusion, bf16[1,2048,768]{2,1,0:T(8,128)(2,1)S(1)} %copy-done, f32[768,768]{1,0:T(8,128)S(1)} %multiply_add_fusion, f32[768,768]{1,0:T(8,128)S(1)} %copy-done.21), kind=kOutput, calls=%fused_computation.6 | convolution fusion | flops 2422603776 | bytes 17301504 | tf_op jit(solution)/shard_map/dot_general | solution.py:15
  269.2 4.8 %all-to-all-start.4 = ((bf16[4,8,24,2048]{3,2,1,0:T(8,128)(2,1)}), bf16[4,8,24,2048]{3,2,1,0:T(8,128)(2,1)}, u32[]{:S(2)}, u32[]{:S(2)}) async-start(bf16[4,8,24,2048]{3,2,1,0:T(8,128)(2,1)} %bitcast.57), calls=%async_computation.4 | async-start | bytes 6291456 | tf_op jit(solution)/shard_map/all_to_all | solution.py:151
  274.1 34.1 %all-to-all-done.4 = bf16[4,8,24,2048]{3,2,1,0:T(8,128)(2,1)} async-done(((bf16[4,8,24,2048]{3,2,1,0:T(8,128)(2,1)}), bf16[4,8,24,2048]{3,2,1,0:T(8,128)(2,1)}, u32[]{:S(2)}, u32[]{:S(2)}) %all-to-all-start.4) | async-done | bytes 3145760 | tf_op jit(solution)/shard_map/all_to_all | solution.py:151
  308.2 3.7 select_reduce_fusion.1
  312.0 1.3 pad_maximum_fusion
  313.3 4.8 %all-to-all-start.5 = ((bf16[2,8,24,2048]{3,2,0,1:T(8,128)(2,1)}), bf16[2,8,24,2048]{3,2,0,1:T(8,128)(2,1)}, u32[]{:S(2)}, u32[]{:S(2)}) async-start(bf16[2,8,24,2048]{3,2,0,1:T(8,128)(2,1)} %pad_maximum_fusion), calls=%async_computation.5 | async-start | bytes 3145728 | tf_op jit(solution)/shard_map/all_to_all | solution.py:156
  318.1 1.6 convolution_multiply_fusion.1
  319.7 0.8 broadcast_multiply_fusion.1
  320.6 0.1 reduce_sum.68
  320.7 11.7 %all_gather.15 = bf16[2,64,2048]{2,1,0:T(8,128)(2,1)S(1)} all-gather(bf16[2,16,2048]{2,1,0:T(8,128)(2,1)S(1)} %copy-done.3), channel_id=1, replica_groups=mesh['dp'=4,'expert'=8] {'dp'}, dimensions={1}, use_global_device_ids=true | all-gather | bytes 655360 | tf_op jit(solution)/shard_map/all_gather | solution.py:174
  332.4 0.7 constant_dynamic-slice_fusion
  333.1 13.8 %reduce-scatter.3.cloned.1.call-done = f32[2,16,768]{2,1,0:T(8,128)} async-done(((f32[2,64,768]{2,1,0:T(8,128)}), f32[2,16,768]{2,1,0:T(8,128)}) %reduce-scatter.3.cloned.1.call-update) | async-done | bytes 98320 | tf_op jit(solution)/shard_map/reduce_scatter | solution.py:167
  346.8 1.7 fusion.51
  348.6 8.9 %all_gather.14 = bf16[2,64,768]{2,1,0:T(8,128)(2,1)S(1)} all-gather(bf16[2,16,768]{2,1,0:T(8,128)(2,1)S(1)} %get-tuple-element.20), channel_id=1, replica_groups=mesh['dp'=4,'expert'=8] {'dp'}, dimensions={1}, use_global_device_ids=true | all-gather | bytes 245760 | tf_op jit(solution)/shard_map/all_gather | solution.py:173
  357.5 0.7 constant_dynamic-slice_fusion.1
  358.2 2.7 copy.64
  360.9 5.0 %gather_fusion.2 = bf16[256,2048]{1,0:T(8,128)(2,1)} fusion(bf16[384,2048]{1,0:T(8,128)(2,1)} %bitcast.52, s32[1024]{0:T(1024)S(1)} %pad_clamp_fusion), kind=kCustom, calls=%fused_computation.4 | custom fusion | bytes 2098176 | tf_op jit(solution)/shard_map/jit(_take)/gather | solution.py:159
  365.8 2.4 fusion.12
  (65 shorter events, 0.5 us)
Async XLA Ops:
  7.2 198.8 %copy-start = (bf16[1,2048,768]{2,1,0:T(8,128)(2,1)S(1)}, bf16[1,2048,768]{2,1,0:T(8,128)(2,1)}, u32[]{:S(2)}) copy-start(bf16[1,2048,768]{2,1,0:T(8,128)(2,1)} %param.22) | copy-start | bytes 9437188
  8.5 0.6 copy-start.9
  8.5 0.6 copy-start.11
  10.5 6.1 %copy-start.6 = (s32[384]{0:T(512)}, s32[384]{0:T(512)S(1)}, u32[]{:S(2)}) copy-start(s32[384]{0:T(512)S(1)} %scatter_custom_fusion) | copy-start | bytes 4612
  19.4 7.2 %copy-start.5 = (bf16[32,2048]{1,0:T(8,128)(2,1)S(1)}, bf16[32,2048]{1,0:T(8,128)(2,1)}, u32[]{:S(2)}) copy-start(bf16[32,2048]{1,0:T(8,128)(2,1)} %param.17) | copy-start | bytes 393220
  19.4 44.4 %all-to-all-start.2 = ((bf16[2,8,24,2048]{3,2,0,1:T(8,128)(2,1)}), bf16[2,8,24,2048]{3,2,0,1:T(8,128)(2,1)}, u32[]{:S(2)}, u32[]{:S(2)}) async-start(bf16[2,8,24,2048]{3,2,0,1:T(8,128)(2,1)} %copy_select_fusion), calls=%async_computation.2 | async-start | bytes 3145728 | tf_op jit(solution)/shard_map/all_to_all | solution.py:96
  29.3 6.4 %copy-start.7 = (pred[2,8,24]{2,0,1:T(4,128)(4,1)S(1)}, pred[2,8,24]{2,0,1:T(4,128)(4,1)}, u32[]{:S(2)}) copy-start(pred[2,8,24]{2,0,1:T(4,128)(4,1)} %copy.59) | copy-start | bytes 1156
  38.5 29.5 %copy-start.8 = (s32[4,8]{1,0:T(4,128)S(1)}, s32[4,8]{1,0:T(4,128)}, u32[]{:S(2)}) copy-start(s32[4,8]{1,0:T(4,128)} %param.20) | copy-start | bytes 388
  63.8 42.1 %all-to-all-start = ((bf16[2,8,24,2048]{3,2,0,1:T(8,128)(2,1)}), bf16[2,8,24,2048]{3,2,0,1:T(8,128)(2,1)}, u32[]{:S(2)}, u32[]{:S(2)}) async-start(bf16[2,8,24,2048]{3,2,0,1:T(8,128)(2,1)} %copy_select_fusion.1), calls=%async_computation | async-start | bytes 3145728 | tf_op jit(solution)/shard_map/all_to_all | solution.py:97
  69.9 39.8 %copy-start.14 = (pred[4,8]{1,0:T(4,128)(4,1)}, pred[4,8]{1,0:T(4,128)(4,1)S(1)}, u32[]{:S(2)}) copy-start(pred[4,8]{1,0:T(4,128)(4,1)S(1)} %get-tuple-element.25) | copy-start | bytes 100
  155.0 6.1 %copy-start.4 = (f32[2,16,768]{2,1,0:T(8,128)S(1)}, f32[2,16,768]{2,1,0:T(8,128)}, u32[]{:S(2)}) copy-start(f32[2,16,768]{2,1,0:T(8,128)} %param.24) | copy-start | bytes 294916
  155.0 55.5 %all-to-all-start.1 = ((bf16[4,8,24,2048]{3,2,1,0:T(8,128)(2,1)}), bf16[4,8,24,2048]{3,2,1,0:T(8,128)(2,1)}, u32[]{:S(2)}, u32[]{:S(2)}) async-start(bf16[4,8,24,2048]{3,2,1,0:T(8,128)(2,1)} %get-tuple-element.32), calls=%async_computation.1 | async-start | bytes 6291456 | tf_op jit(solution)/shard_map/all_to_all | solution.py:113
  159.8 84.1 %reduce-scatter.5.cloned.1.call-start = ((), (), s32[]{:S(2)}) async-start(), calls=%async_computation.9 | async-start | bytes 1310720 | tf_op jit(solution)/shard_map/reduce_scatter | solution.py:168
  199.0 15.8 %copy-start.16 = (f32[2]{0:T(128)}, f32[2]{0:T(128)S(1)}, u32[]{:S(2)}) copy-start(f32[2]{0:T(128)S(1)} %compare_convert_fusion) | copy-start | bytes 28
  199.0 7.0 %copy-start.1 = (bf16[4,8,24,2048]{3,2,1,0:T(8,128)(2,1)S(1)}, bf16[4,8,24,2048]{3,2,1,0:T(8,128)(2,1)}, u32[]{:S(2)}) copy-start(bf16[4,8,24,2048]{3,2,1,0:T(8,128)(2,1)} %all_to_all.30) | copy-start | bytes 9437188
  204.6 1.4 copy-start.20
  256.5 3.1 copy-start.2
  256.5 3.7 copy-start.21
  256.5 4.0 %copy-start.22 = (f32[768,768]{1,0:T(8,128)S(1)}, f32[768,768]{1,0:T(8,128)}, u32[]{:S(2)}) copy-start(f32[768,768]{1,0:T(8,128)} %get-tuple-element.35) | copy-start | bytes 7077892
  259.6 2.1 copy-start.19
  269.2 4.8 %copy-start.15 = (pred[4,8]{1,0:T(4,128)(4,1)S(1)}, pred[4,8]{1,0:T(4,128)(4,1)}, u32[]{:S(2)}) copy-start(pred[4,8]{1,0:T(4,128)(4,1)} %copy-done.14) | copy-start | bytes 100
  269.2 4.8 %copy-start.18 = (pred[4]{0:T(512)(128)(4,1)S(1)}, pred[4]{0:T(512)(128)(4,1)}, u32[]{:S(2)}) copy-start(pred[4]{0:T(512)(128)(4,1)} %get-tuple-element.12) | copy-start | bytes 16
  269.2 39.0 %copy-start.13 = (pred[4,8]{1,0:T(4,128)(4,1)S(1)}, pred[4,8]{1,0:T(4,128)(4,1)}, u32[]{:S(2)}) copy-start(pred[4,8]{1,0:T(4,128)(4,1)} %get-tuple-element.24) | copy-start | bytes 100
  269.2 39.0 %all-to-all-start.4 = ((bf16[4,8,24,2048]{3,2,1,0:T(8,128)(2,1)}), bf16[4,8,24,2048]{3,2,1,0:T(8,128)(2,1)}, u32[]{:S(2)}, u32[]{:S(2)}) async-start(bf16[4,8,24,2048]{3,2,1,0:T(8,128)(2,1)} %bitcast.57), calls=%async_computation.4 | async-start | bytes 6291456 | tf_op jit(solution)/shard_map/all_to_all | solution.py:151
  313.2 6.4 %copy-start.17 = (f32[2]{0:T(128)S(1)}, f32[2]{0:T(128)}, u32[]{:S(2)}) copy-start(f32[2]{0:T(128)} %copy-done.16) | copy-start | bytes 28
  313.2 7.3 %copy-start.10 = (s32[256]{0:T(256)S(1)}, s32[256]{0:T(256)}, u32[]{:S(2)}) copy-start(s32[256]{0:T(256)} %copy-done.9) | copy-start | bytes 3076
  313.2 7.4 %copy-start.12 = (s32[256,1]{0,1:T(1,128)S(1)}, s32[256,1]{0,1:T(1,128)}, u32[]{:S(2)}) copy-start(s32[256,1]{0,1:T(1,128)} %copy-done.11) | copy-start | bytes 3076
  313.2 7.5 %copy-start.3 = (bf16[2,16,2048]{2,1,0:T(8,128)(2,1)S(1)}, bf16[2,16,2048]{2,1,0:T(8,128)(2,1)}, u32[]{:S(2)}) copy-start(bf16[2,16,2048]{2,1,0:T(8,128)(2,1)} %get-tuple-element.16) | copy-start | bytes 393220
  313.3 44.9 %all-to-all-start.5 = ((bf16[2,8,24,2048]{3,2,0,1:T(8,128)(2,1)}), bf16[2,8,24,2048]{3,2,0,1:T(8,128)(2,1)}, u32[]{:S(2)}, u32[]{:S(2)}) async-start(bf16[2,8,24,2048]{3,2,0,1:T(8,128)(2,1)} %pad_maximum_fusion), calls=%async_computation.5 | async-start | bytes 3145728 | tf_op jit(solution)/shard_map/all_to_all | solution.py:156
  318.0 28.8 %reduce-scatter.3.cloned.1.call-start = ((), (), s32[]{:S(2)}) async-start(), calls=%async_computation.8 | async-start | bytes 491520 | tf_op jit(solution)/shard_map/reduce_scatter | solution.py:167
Sparse Core Ops, SparseCore 0:
  217.1 26.6 reduce-scatter.4
  321.6 25.1 reduce-scatter.2
where the time goes:
time: 376 us; the launch traced here: 375 us
  waiting for transfers between devices  125 us (33%)
  blocking collectives  109 us (29%)
  local copies, waits for them, and re-layouts  37.7 us (10%)
  matrix products  33.9 us (9%)
  other arithmetic  29.3 us (8%)
  starting transfers between devices  25.2 us (7%)
  between operations  15.1 us (4%)
    all_to_all x1, blocking collectives, per_device(): lax.all_to_all(picked_input, 'dp', split_axis=0, concat_axis=0, tiled=True)  39.9 us
    all_gather x1, blocking collectives, per_device(): lax.all_gather(adapter_in.astype(jnp.bfloat16), 'dp', axis=1, tiled=True)  37.8 us
    all_to_all x1, waiting for transfers between devices, per_device(): lax.all_to_all(back_block, 'dp', split_axis=0, concat_axis=0, tiled=True)  34.1 us
    all_to_all x1, waiting for transfers between devices, per_device(): lax.all_to_all(col_grad, 'expert', split_axis=1, concat_axis=1, tiled=True)  32.2 us
    all_to_all x1, waiting for transfers between devices, per_device(): lax.all_to_all(col_input, 'expert', split_axis=1, concat_axis=1, tiled=True)  25.2 us
    dot_general x6, matrix products, contract_product(): lax.dot_general(left, right, (((left_dim,), (right_dim,)), ((), ())), pre...  23.4 us
    reduce_scatter x1, waiting for transfers between devices, per_device(): lax.psum_scatter(placed_out, 'dp', scatter_dimension=1, tiled=True)  20 us
    reduce_scatter x1, waiting for transfers between devices, per_device(): lax.psum_scatter(placed_in, 'dp', scatter_dimension=1, tiled=True)  13.8 us
  transfers between devices with their start and end apart: 7, of which 5 were waited for; matrix products, arithmetic and copies ran while one was open for 11% of the time, Pallas kernels for 0%

commit v1 on v0

--- a/solution.py
+++ b/solution.py
@@ -112,8 +112,12 @@
         lax.all_to_all(picked_input, "dp", split_axis=0, concat_axis=0, tiled=True),
         lax.all_to_all(picked_grad, "dp", split_axis=0, concat_axis=0, tiled=True),
     )
+    push_gates_on = lambda m: jnp.concatenate(
+        jax.lax.all_to_all(jnp.stack([m for _ in range(jax.lax.axis_size("dp"))]), "dp", 0, 0),
+        axis=1,
+    )
     fetched_in, fetched_out = (
-        lax.all_gather(adapter_in.astype(jnp.bfloat16), "dp", axis=1, tiled=True),
+        push_gates_on(adapter_in.astype(jnp.bfloat16)),
         lax.all_gather(adapter_out.astype(jnp.bfloat16), "dp", axis=1, tiled=True),
     )
     hosted_local = slot_expert[dp_index, column_index] - local_experts * column_index

time: 376 us -> 367 us (0.976)
  blocking collectives: 109 us -> 72.5 us
  waiting for transfers between devices: 125 us -> 146 us
    all_gather x1 -> x0, blocking collectives: 37.8 us -> none  [per_device(): lax.all_gather(adapter_in.astype(jnp.bfloat16), 'dp', axis=1, tiled=True)]
    all_to_all x1, waiting for transfers between devices: 0.01 us -> 21.1 us  [per_device(): lax.all_to_all(picked_grad, 'dp', split_axis=0, concat_axis=0, tiled=True)]
  transfers between devices with their start and end apart: 7 -> 8, of which waited for: 5 -> 6; matrix products, arithmetic and copies ran while one was open for 11% -> 14% of each run, Pallas kernels for 0% -> 0%
where the time goes in v1:
time: 367 us; the launch traced here: 366 us
  waiting for transfers between devices  146 us (40%)
  blocking collectives  72.5 us (20%)
  local copies, waits for them, and re-layouts  38.4 us (10%)
  matrix products  33.9 us (9%)
  other arithmetic  30.7 us (8%)
  starting transfers between devices  28.9 us (8%)
  between operations  15.1 us (4%)
    all_to_all x1, blocking collectives, per_device(): lax.all_to_all(picked_input, 'dp', split_axis=0, concat_axis=0, tiled=True)  41.6 us
    all_to_all x1, waiting for transfers between devices, per_device(): lax.all_to_all(back_block, 'dp', split_axis=0, concat_axis=0, tiled=True)  34.1 us
    all_to_all x1, waiting for transfers between devices, per_device(): lax.all_to_all(col_grad, 'expert', split_axis=1, concat_axis=1, tiled=True)  32.1 us
    all_to_all x1, waiting for transfers between devices, per_device(): lax.all_to_all(col_input, 'expert', split_axis=1, concat_axis=1, tiled=True)  25.3 us
    dot_general x6, matrix products, contract_product(): lax.dot_general(left, right, (((left_dim,), (right_dim,)), ((), ())), pre...  23.3 us
    all_to_all x1, waiting for transfers between devices, per_device(): lax.all_to_all(picked_grad, 'dp', split_axis=0, concat_axis=0, tiled=True)  21.1 us
    reduce_scatter x1, waiting for transfers between devices, per_device(): lax.psum_scatter(placed_out, 'dp', scatter_dimension=1, tiled=True)  20 us
    reduce_scatter x1, waiting for transfers between devices, per_device(): lax.psum_scatter(placed_in, 'dp', scatter_dimension=1, tiled=True)  13.7 us
  transfers between devices with their start and end apart: 8, of which 6 were waited for; matrix products, arithmetic and copies ran while one was open for 14% of the time, Pallas kernels for 0%

profile of v1, /device:TPU:0, one launch (start us, length us, event | category | flops | bytes accessed | tf_op | source)
XLA Modules:
  0.0 365.8 jit_solution(11812696293812238434)
XLA Ops:
  7.2 0.9 copy.55
  8.3 0.2 convert_reduce_fusion
  8.5 0.5 copy-done.10
  9.1 1.4 scatter_custom_fusion
  10.5 0.1 broadcast_in_dim.106
  10.6 6.0 %gather_fusion.1 = bf16[384,2048]{1,0:T(8,128)(2,1)} fusion(bf16[32,2048]{1,0:T(8,128)(2,1)} %param.16, s32[1024]{0:T(1024)S(1)} %pad_clamp_fusion.1), kind=kCustom, calls=%fused_computation.3 | custom fusion | bytes 3147264 | tf_op jit(solution)/shard_map/jit(_take)/gather | solution.py:39
  16.6 2.8 copy_select_fusion
  19.4 6.5 %all-to-all-start.3 = ((bf16[2,8,24,2048]{3,2,0,1:T(8,128)(2,1)}), bf16[2,8,24,2048]{3,2,0,1:T(8,128)(2,1)}, u32[]{:S(2)}, u32[]{:S(2)}) async-start(bf16[2,8,24,2048]{3,2,0,1:T(8,128)(2,1)} %copy_select_fusion), calls=%async_computation.3 | async-start | bytes 3145728 | tf_op jit(solution)/shard_map/all_to_all | solution.py:96
  25.9 0.1 broadcast_in_dim.101
  26.0 0.6 copy.61
  26.6 0.8 copy.62
  27.4 0.7 add_select_fusion.3
  28.1 1.2 fusion.9
  29.3 6.4 %gather_fusion = bf16[384,2048]{1,0:T(8,128)(2,1)} fusion(bf16[256,2048]{1,0:T(8,128)(2,1)} %fusion.9, s32[1024]{0:T(1024)S(1)} %pad_clamp_fusion.3), kind=kCustom, calls=%fused_computation.2 | custom fusion | bytes 3147264 | tf_op jit(solution)/shard_map/jit(_take)/gather | solution.py:40
  35.8 2.7 copy_select_fusion.1
  38.5 25.3 %all-to-all-done.3 = bf16[2,8,24,2048]{3,2,0,1:T(8,128)(2,1)} async-done(((bf16[2,8,24,2048]{3,2,0,1:T(8,128)(2,1)}), bf16[2,8,24,2048]{3,2,0,1:T(8,128)(2,1)}, u32[]{:S(2)}, u32[]{:S(2)}) %all-to-all-start.3) | async-done | bytes 1572896 | tf_op jit(solution)/shard_map/all_to_all | solution.py:96
  63.8 4.3 %all-to-all-start = ((bf16[2,8,24,2048]{3,2,0,1:T(8,128)(2,1)}), bf16[2,8,24,2048]{3,2,0,1:T(8,128)(2,1)}, u32[]{:S(2)}, u32[]{:S(2)}) async-start(bf16[2,8,24,2048]{3,2,0,1:T(8,128)(2,1)} %copy_select_fusion.1), calls=%async_computation | async-start | bytes 3145728 | tf_op jit(solution)/shard_map/all_to_all | solution.py:97
  68.1 0.2 fusion.42
  68.3 0.7 compare_reduce_fusion.1
  69.0 0.2 convert_reduce_fusion.1
  69.2 0.7 broadcast_and_fusion
  69.9 3.8 %gather_fusion.4 = bf16[4,8,24,2048]{3,2,1,0:T(8,128)(2,1)} fusion(bf16[2,8,24,2048]{3,2,0,1:T(8,128)(2,1)} %all-to-all-done.3, s32[1024]{0:T(1024)S(1)} %pad_clamp_fusion.2), kind=kCustom, calls=%fused_computation.1.clone | custom fusion | bytes 6291472 | tf_op jit(solution)/shard_map/jit(_take)/gather | solution.py:109
  73.7 32.1 %all-to-all-done = bf16[2,8,24,2048]{3,2,0,1:T(8,128)(2,1)} async-done(((bf16[2,8,24,2048]{3,2,0,1:T(8,128)(2,1)}), bf16[2,8,24,2048]{3,2,0,1:T(8,128)(2,1)}, u32[]{:S(2)}, u32[]{:S(2)}) %all-to-all-start) | async-done | bytes 1572896 | tf_op jit(solution)/shard_map/all_to_all | solution.py:97
  105.9 0.7 stack.16
  106.6 3.7 %all-to-all-start.2 = ((bf16[4,2,16,768]{3,2,1,0:T(8,128)(2,1)}), bf16[4,2,16,768]{3,2,1,0:T(8,128)(2,1)S(1)}, u32[]{:S(2)}, u32[]{:S(2)}) async-start(bf16[4,2,16,768]{3,2,1,0:T(8,128)(2,1)} %stack.16), calls=%async_computation.2 | async-start | bytes 393216 | tf_op jit(solution)/shard_map/all_to_all | solution.py:116
  110.3 3.8 %gather_fusion.3 = bf16[4,8,24,2048]{3,2,1,0:T(8,128)(2,1)} fusion(bf16[2,8,24,2048]{3,2,0,1:T(8,128)(2,1)} %all-to-all-done, s32[1024]{0:T(1024)S(1)} %pad_clamp_fusion.2), kind=kCustom, calls=%fused_computation.clone | custom fusion | bytes 6291472 | tf_op jit(solution)/shard_map/jit(_take)/gather | solution.py:110
  114.1 6.2 %select_select_fusion.1 = (bf16[4,8,24,2048]{3,2,1,0:T(8,128)(2,1)}, bf16[4,8,24,2048]{3,2,1,0:T(8,128)(2,1)}) fusion(bf16[4,8,24,2048]{3,2,1,0:T(8,128)(2,1)} %gather_fusion.3, pred[4]{0:T(512)(128)(4,1)S(1)} %get-tuple-element.26, pred[4,8]{1,0:T(4,128)(4,1)S(1)} %get-tuple-element.25, bf16[4,8,24,2048]{3,2,1,0:T(8,128)(2,1)} %gather_fusion.4), kind=kLoop, calls=%fused_computation.17 | loop fusion | flops 6291456 | bytes 12582948 | tf_op jit(solution)/shard_map/jit(_where)/select_n | solution.py:110
  120.3 41.6 %all_to_all.35 = bf16[4,8,24,2048]{3,2,1,0:T(8,128)(2,1)} all-to-all(bf16[4,8,24,2048]{3,2,1,0:T(8,128)(2,1)} %get-tuple-element.33), channel_id=1, replica_groups=mesh['dp'=4,'expert'=8] {'dp'}, dimensions={0} | all-to-all | bytes 6291456 | tf_op jit(solution)/shard_map/all_to_all | solution.py:112
  162.0 4.6 %all-to-all-start.1 = ((bf16[4,8,24,2048]{3,2,1,0:T(8,128)(2,1)}), bf16[4,8,24,2048]{3,2,1,0:T(8,128)(2,1)}, u32[]{:S(2)}, u32[]{:S(2)}) async-start(bf16[4,8,24,2048]{3,2,1,0:T(8,128)(2,1)} %get-tuple-element.32), calls=%async_computation.1 | async-start | bytes 6291456 | tf_op jit(solution)/shard_map/all_to_all | solution.py:113
  166.6 0.2 reduce-scatter.5.cloned.1.call-start
  166.8 0.6 dynamic_slice.24
  168.1 0.5 compare_convert_fusion
  168.6 5.6 %fusion.2 = f32[768,768]{1,0:T(8,128)S(1)} fusion(bf16[768,2048]{1,0:T(8,128)(2,1)} %bitcast.58, bf16[1,2048,768]{2,1,0:T(8,128)(2,1)} %param.21), kind=kOutput, calls=%fused_computation.9 | convolution fusion | flops 2415919104 | bytes 8650752 | tf_op jit(solution)/shard_map/dot_general | solution.py:131
  174.2 1.4 copy-done.21
  175.7 4.5 %multiply_convert_fusion = (bf16[768,768]{1,0:T(8,128)(2,1)}, f32[768,768]{1,0:T(8,128)}) fusion(f32[768,768]{1,0:T(8,128)S(1)} %fusion.2, bf16[768,2048]{1,0:T(8,128)(2,1)S(1)} %bitcast.59, bf16[1,2048,768]{2,1,0:T(8,128)(2,1)S(1)} %copy-done), kind=kOutput, calls=%fused_computation.20 | convolution fusion | flops 2419458048 | bytes 12189696 | tf_op jit(solution)/shard_map/dot_general | solution.py:132
  180.2 21.1 %all-to-all-done.1 = bf16[4,8,24,2048]{3,2,1,0:T(8,128)(2,1)} async-done(((bf16[4,8,24,2048]{3,2,1,0:T(8,128)(2,1)}), bf16[4,8,24,2048]{3,2,1,0:T(8,128)(2,1)}, u32[]{:S(2)}, u32[]{:S(2)}) %all-to-all-start.1) | async-done | bytes 3145760 | tf_op jit(solution)/shard_map/all_to_all | solution.py:113
  201.3 4.3 %convolution_multiply_fusion = f32[64,2048]{1,0:T(8,128)} fusion(bf16[768,2048]{1,0:T(8,128)(2,1)} %bitcast.4, bf16[768,768]{1,0:T(8,128)(2,1)} %get-tuple-element.34, bf16[2,64,768]{2,1,0:T(8,128)(2,1)S(1)} %bitcast.63, s32[]{:T(128)S(6)} %select_n.159), kind=kOutput, calls=%fused_computation.25 | convolution fusion | flops 277004288 | bytes 4947972 | tf_op jit(solution)/shard_map/dot_general | solution.py:15
  205.6 2.2 broadcast_multiply_fusion
  207.8 6.9 %fusion.7 = f32[768,768]{1,0:T(8,128)} fusion(bf16[768,2048]{1,0:T(8,128)(2,1)} %bitcast.4, bf16[1,768,2048]{2,1,0:T(8,128)(2,1)} %param.23), kind=kOutput, calls=%fused_computation.14 | convolution fusion | flops 2415919104 | bytes 8650752 | tf_op jit(solution)/shard_map/dot_general | solution.py:15
  214.7 20.0 %reduce-scatter.5.cloned.1.call-done = f32[2,16,2048]{2,1,0:T(8,128)} async-done(((f32[2,64,2048]{2,1,0:T(8,128)}), f32[2,16,2048]{2,1,0:T(8,128)}) %reduce-scatter.5.cloned.1.call-update) | async-done | bytes 262160 | tf_op jit(solution)/shard_map/reduce_scatter | solution.py:172
  234.7 2.3 fusion.49
  237.0 10.2 %all_gather.9 = bf16[2,64,2048]{2,1,0:T(8,128)(2,1)S(1)} all-gather(bf16[2,16,2048]{2,1,0:T(8,128)(2,1)S(1)} %get-tuple-element.30), channel_id=1, replica_groups=mesh['dp'=4,'expert'=8] {'dp'}, dimensions={1}, use_global_device_ids=true | all-gather | bytes 655360 | tf_op jit(solution)/shard_map/all_gather | solution.py:121
  247.3 3.1 convolution_convert_fusion.1
  250.4 0.5 multiply_add_fusion
  250.9 0.4 copy-done.23
  251.3 1.2 copy-done.20
  252.5 3.3 fusion
  255.8 4.1 %add_convert_fusion = bf16[768,2048]{1,0:T(8,128)(2,1)} fusion(f32[768,2048]{1,0:T(8,128)S(1)} %fusion, bf16[1,2048,768]{2,1,0:T(8,128)(2,1)S(1)} %copy-done, f32[768,768]{1,0:T(8,128)S(1)} %multiply_add_fusion, f32[768,768]{1,0:T(8,128)S(1)} %copy-done.22), kind=kOutput, calls=%fused_computation.6 | convolution fusion | flops 2422603776 | bytes 17301504 | tf_op jit(solution)/shard_map/dot_general | solution.py:15
  259.9 4.8 %all-to-all-start.5 = ((bf16[4,8,24,2048]{3,2,1,0:T(8,128)(2,1)}), bf16[4,8,24,2048]{3,2,1,0:T(8,128)(2,1)}, u32[]{:S(2)}, u32[]{:S(2)}) async-start(bf16[4,8,24,2048]{3,2,1,0:T(8,128)(2,1)} %bitcast.60), calls=%async_computation.5 | async-start | bytes 6291456 | tf_op jit(solution)/shard_map/all_to_all | solution.py:155
  264.8 34.1 %all-to-all-done.5 = bf16[4,8,24,2048]{3,2,1,0:T(8,128)(2,1)} async-done(((bf16[4,8,24,2048]{3,2,1,0:T(8,128)(2,1)}), bf16[4,8,24,2048]{3,2,1,0:T(8,128)(2,1)}, u32[]{:S(2)}, u32[]{:S(2)}) %all-to-all-start.5) | async-done | bytes 3145760 | tf_op jit(solution)/shard_map/all_to_all | solution.py:155
  298.9 3.7 %select_reduce_fusion.1 = (bf16[8,24,2048]{2,1,0:T(8,128)(2,1)S(1)}, bf16[8,24,2048]{2,1,0:T(8,128)(2,1)S(1)}) fusion(bf16[4,8,24,2048]{3,2,1,0:T(8,128)(2,1)} %all-to-all-done.5, pred[4,8]{1,0:T(4,128)(4,1)S(1)} %broadcast_and_fusion.1, pred[4,8]{1,0:T(4,128)(4,1)S(1)} %copy-done.14), kind=kLoop, calls=%fused_computation.19 | loop fusion | flops 5505024 | bytes 4718656 | tf_op jit(solution)/shard_map/reduce_sum | solution.py:159
  302.7 1.3 pad_maximum_fusion
  304.0 4.7 %all-to-all-start.6 = ((bf16[2,8,24,2048]{3,2,0,1:T(8,128)(2,1)}), bf16[2,8,24,2048]{3,2,0,1:T(8,128)(2,1)}, u32[]{:S(2)}, u32[]{:S(2)}) async-start(bf16[2,8,24,2048]{3,2,0,1:T(8,128)(2,1)} %pad_maximum_fusion), calls=%async_computation.6 | async-start | bytes 3145728 | tf_op jit(solution)/shard_map/all_to_all | solution.py:160
  308.8 1.6 convolution_multiply_fusion.1
  310.4 0.8 broadcast_multiply_fusion.1
  311.4 11.7 %all_gather.11 = bf16[2,64,2048]{2,1,0:T(8,128)(2,1)S(1)} all-gather(bf16[2,16,2048]{2,1,0:T(8,128)(2,1)S(1)} %copy-done.3), channel_id=1, replica_groups=mesh['dp'=4,'expert'=8] {'dp'}, dimensions={1}, use_global_device_ids=true | all-gather | bytes 655360 | tf_op jit(solution)/shard_map/all_gather | solution.py:178
  323.1 0.7 constant_dynamic-slice_fusion
  323.8 13.7 %reduce-scatter.3.cloned.1.call-done = f32[2,16,768]{2,1,0:T(8,128)} async-done(((f32[2,64,768]{2,1,0:T(8,128)}), f32[2,16,768]{2,1,0:T(8,128)}) %reduce-scatter.3.cloned.1.call-update) | async-done | bytes 98320 | tf_op jit(solution)/shard_map/reduce_scatter | solution.py:171
  337.6 1.7 fusion.51
  339.3 8.9 %all_gather.10 = bf16[2,64,768]{2,1,0:T(8,128)(2,1)S(1)} all-gather(bf16[2,16,768]{2,1,0:T(8,128)(2,1)S(1)} %get-tuple-element.20), channel_id=1, replica_groups=mesh['dp'=4,'expert'=8] {'dp'}, dimensions={1}, use_global_device_ids=true | all-gather | bytes 245760 | tf_op jit(solution)/shard_map/all_gather | solution.py:177
  348.2 0.7 constant_dynamic-slice_fusion.1
  348.9 2.7 copy.67
  351.6 5.0 %gather_fusion.2 = bf16[256,2048]{1,0:T(8,128)(2,1)} fusion(bf16[384,2048]{1,0:T(8,128)(2,1)} %bitcast.55, s32[1024]{0:T(1024)S(1)} %pad_clamp_fusion), kind=kCustom, calls=%fused_computation.4 | custom fusion | bytes 2098176 | tf_op jit(solution)/shard_map/jit(_take)/gather | solution.py:163
  356.6 2.4 fusion.12
  (70 shorter events, 0.8 us)
Async XLA Ops:
  7.2 168.5 %copy-start = (bf16[1,2048,768]{2,1,0:T(8,128)(2,1)S(1)}, bf16[1,2048,768]{2,1,0:T(8,128)(2,1)}, u32[]{:S(2)}) copy-start(bf16[1,2048,768]{2,1,0:T(8,128)(2,1)} %param.22) | copy-start | bytes 9437188
  8.5 0.6 copy-start.10
  8.5 0.6 copy-start.12
  10.5 6.1 %copy-start.7 = (s32[384]{0:T(512)}, s32[384]{0:T(512)S(1)}, u32[]{:S(2)}) copy-start(s32[384]{0:T(512)S(1)} %scatter_custom_fusion) | copy-start | bytes 4612
  19.4 7.2 %copy-start.6 = (bf16[32,2048]{1,0:T(8,128)(2,1)S(1)}, bf16[32,2048]{1,0:T(8,128)(2,1)}, u32[]{:S(2)}) copy-start(bf16[32,2048]{1,0:T(8,128)(2,1)} %param.17) | copy-start | bytes 393220
  19.4 44.4 %all-to-all-start.3 = ((bf16[2,8,24,2048]{3,2,0,1:T(8,128)(2,1)}), bf16[2,8,24,2048]{3,2,0,1:T(8,128)(2,1)}, u32[]{:S(2)}, u32[]{:S(2)}) async-start(bf16[2,8,24,2048]{3,2,0,1:T(8,128)(2,1)} %copy_select_fusion), calls=%async_computation.3 | async-start | bytes 3145728 | tf_op jit(solution)/shard_map/all_to_all | solution.py:96
  29.3 6.4 %copy-start.8 = (pred[2,8,24]{2,0,1:T(4,128)(4,1)S(1)}, pred[2,8,24]{2,0,1:T(4,128)(4,1)}, u32[]{:S(2)}) copy-start(pred[2,8,24]{2,0,1:T(4,128)(4,1)} %copy.61) | copy-start | bytes 1156
  38.5 29.6 %copy-start.4 = (f32[2,16,768]{2,1,0:T(8,128)S(1)}, f32[2,16,768]{2,1,0:T(8,128)}, u32[]{:S(2)}) copy-start(f32[2,16,768]{2,1,0:T(8,128)} %param.24) | copy-start | bytes 294916
  38.5 29.6 %copy-start.9 = (s32[4,8]{1,0:T(4,128)S(1)}, s32[4,8]{1,0:T(4,128)}, u32[]{:S(2)}) copy-start(s32[4,8]{1,0:T(4,128)} %param.20) | copy-start | bytes 388
  63.8 42.1 %all-to-all-start = ((bf16[2,8,24,2048]{3,2,0,1:T(8,128)(2,1)}), bf16[2,8,24,2048]{3,2,0,1:T(8,128)(2,1)}, u32[]{:S(2)}, u32[]{:S(2)}) async-start(bf16[2,8,24,2048]{3,2,0,1:T(8,128)(2,1)} %copy_select_fusion.1), calls=%async_computation | async-start | bytes 3145728 | tf_op jit(solution)/shard_map/all_to_all | solution.py:97
  69.9 44.2 %copy-start.15 = (pred[4,8]{1,0:T(4,128)(4,1)}, pred[4,8]{1,0:T(4,128)(4,1)S(1)}, u32[]{:S(2)}) copy-start(pred[4,8]{1,0:T(4,128)(4,1)S(1)} %get-tuple-element.25) | copy-start | bytes 100
  106.6 13.8 %all-to-all-start.2 = ((bf16[4,2,16,768]{3,2,1,0:T(8,128)(2,1)}), bf16[4,2,16,768]{3,2,1,0:T(8,128)(2,1)S(1)}, u32[]{:S(2)}, u32[]{:S(2)}) async-start(bf16[4,2,16,768]{3,2,1,0:T(8,128)(2,1)} %stack.16), calls=%async_computation.2 | async-start | bytes 393216 | tf_op jit(solution)/shard_map/all_to_all | solution.py:116
  162.0 39.3 %all-to-all-start.1 = ((bf16[4,8,24,2048]{3,2,1,0:T(8,128)(2,1)}), bf16[4,8,24,2048]{3,2,1,0:T(8,128)(2,1)}, u32[]{:S(2)}, u32[]{:S(2)}) async-start(bf16[4,8,24,2048]{3,2,1,0:T(8,128)(2,1)} %get-tuple-element.32), calls=%async_computation.1 | async-start | bytes 6291456 | tf_op jit(solution)/shard_map/all_to_all | solution.py:113
  166.6 68.1 %reduce-scatter.5.cloned.1.call-start = ((), (), s32[]{:S(2)}) async-start(), calls=%async_computation.10 | async-start | bytes 1310720 | tf_op jit(solution)/shard_map/reduce_scatter | solution.py:172
  168.6 7.1 %copy-start.1 = (bf16[4,8,24,2048]{3,2,1,0:T(8,128)(2,1)S(1)}, bf16[4,8,24,2048]{3,2,1,0:T(8,128)(2,1)}, u32[]{:S(2)}) copy-start(bf16[4,8,24,2048]{3,2,1,0:T(8,128)(2,1)} %all_to_all.35) | copy-start | bytes 9437188
  174.2 1.5 copy-start.21
  201.3 4.3 %copy-start.17 = (f32[2]{0:T(128)S(1)}, f32[2]{0:T(128)}, u32[]{:S(2)}) copy-start(f32[2]{0:T(128)} %compare_convert_fusion) | copy-start | bytes 28
  247.3 3.1 copy-start.2
  247.3 3.7 %copy-start.22 = (f32[768,768]{1,0:T(8,128)S(1)}, f32[768,768]{1,0:T(8,128)}, u32[]{:S(2)}) copy-start(f32[768,768]{1,0:T(8,128)} %copy-done.21) | copy-start | bytes 7077892
  247.3 4.0 %copy-start.23 = (f32[768,768]{1,0:T(8,128)S(1)}, f32[768,768]{1,0:T(8,128)}, u32[]{:S(2)}) copy-start(f32[768,768]{1,0:T(8,128)} %get-tuple-element.35) | copy-start | bytes 7077892
  250.4 2.1 copy-start.20
  259.9 4.8 %copy-start.16 = (pred[4,8]{1,0:T(4,128)(4,1)S(1)}, pred[4,8]{1,0:T(4,128)(4,1)}, u32[]{:S(2)}) copy-start(pred[4,8]{1,0:T(4,128)(4,1)} %copy-done.15) | copy-start | bytes 100
  259.9 4.8 %copy-start.19 = (pred[4]{0:T(512)(128)(4,1)S(1)}, pred[4]{0:T(512)(128)(4,1)}, u32[]{:S(2)}) copy-start(pred[4]{0:T(512)(128)(4,1)} %get-tuple-element.12) | copy-start | bytes 16
  259.9 39.0 %copy-start.14 = (pred[4,8]{1,0:T(4,128)(4,1)S(1)}, pred[4,8]{1,0:T(4,128)(4,1)}, u32[]{:S(2)}) copy-start(pred[4,8]{1,0:T(4,128)(4,1)} %get-tuple-element.24) | copy-start | bytes 100
  259.9 39.0 %all-to-all-start.5 = ((bf16[4,8,24,2048]{3,2,1,0:T(8,128)(2,1)}), bf16[4,8,24,2048]{3,2,1,0:T(8,128)(2,1)}, u32[]{:S(2)}, u32[]{:S(2)}) async-start(bf16[4,8,24,2048]{3,2,1,0:T(8,128)(2,1)} %bitcast.60), calls=%async_computation.5 | async-start | bytes 6291456 | tf_op jit(solution)/shard_map/all_to_all | solution.py:155
  304.0 6.4 %copy-start.18 = (f32[2]{0:T(128)S(1)}, f32[2]{0:T(128)}, u32[]{:S(2)}) copy-start(f32[2]{0:T(128)} %compare_convert_fusion) | copy-start | bytes 28
  304.0 7.3 %copy-start.11 = (s32[256]{0:T(256)S(1)}, s32[256]{0:T(256)}, u32[]{:S(2)}) copy-start(s32[256]{0:T(256)} %copy-done.10) | copy-start | bytes 3076
  304.0 7.4 %copy-start.13 = (s32[256,1]{0,1:T(1,128)S(1)}, s32[256,1]{0,1:T(1,128)}, u32[]{:S(2)}) copy-start(s32[256,1]{0,1:T(1,128)} %copy-done.12) | copy-start | bytes 3076
  304.0 7.4 %copy-start.3 = (bf16[2,16,2048]{2,1,0:T(8,128)(2,1)S(1)}, bf16[2,16,2048]{2,1,0:T(8,128)(2,1)}, u32[]{:S(2)}) copy-start(bf16[2,16,2048]{2,1,0:T(8,128)(2,1)} %get-tuple-element.16) | copy-start | bytes 393220
  304.0 44.9 %all-to-all-start.6 = ((bf16[2,8,24,2048]{3,2,0,1:T(8,128)(2,1)}), bf16[2,8,24,2048]{3,2,0,1:T(8,128)(2,1)}, u32[]{:S(2)}, u32[]{:S(2)}) async-start(bf16[2,8,24,2048]{3,2,0,1:T(8,128)(2,1)} %pad_maximum_fusion), calls=%async_computation.6 | async-start | bytes 3145728 | tf_op jit(solution)/shard_map/all_to_all | solution.py:160
  308.7 28.8 %copy-start.5 = (f32[2,16,768]{2,1,0:T(8,128)S(1)}, f32[2,16,768]{2,1,0:T(8,128)}, u32[]{:S(2)}) copy-start(f32[2,16,768]{2,1,0:T(8,128)} %param.24) | copy-start | bytes 294916
  308.7 28.8 %reduce-scatter.3.cloned.1.call-start = ((), (), s32[]{:S(2)}) async-start(), calls=%async_computation.9 | async-start | bytes 491520 | tf_op jit(solution)/shard_map/reduce_scatter | solution.py:171
Sparse Core Ops, SparseCore 0:
  208.0 26.7 reduce-scatter.4
  312.3 25.1 reduce-scatter.2
